TPU v7x, 32 devices: a whole 2x2x4 slice. The times are simulated.
32 devices in a mesh: groups: 2 (over y), tile: 4 (over z), pair: 2 (over x), sub: 2 (over core).
Axes of the slice: x: 2, y: 2, z: 4, core: 2. Of those that a mesh axis runs over, the one named last changes fastest.
Arguments:
- ref_chips: bfloat16 [4, 256, 4096], P(('groups', 'pair'), ('tile', 'sub')), parts along dimension 0, may hold values from -300 to 700
- search_windows: bfloat16 [4, 512, 16384], P(('groups', 'pair'), ('tile', 'sub')), parts along dimension 0, may hold values from -300 to 700
- dest_block: int32 [4, 512, 1], P(('groups', 'pair'), ('tile', 'sub')), parts along dimension 0, may hold values from 0 to 7; in each aligned block of 64 rows (0 to 63, 64 to 127, ..., all dimensions but the last counted through in order) at most 16 rows name the same one
- dest_slot: int32 [4, 512], P(('groups', 'pair'), ('tile', 'sub')), parts along dimension 0, may hold values from 0 to 31
Outputs:
- smoothed_scores: float32 [4, 256, 4096], P(('groups', 'pair'), ('tile', 'sub')), parts along dimension 0
There are 2 independent parts, one for each index of `groups`. A program takes and returns all parts, laid end to end along the dimension named above; each array names one. Nothing has to cross between parts.
Inputs may be any that keep to these rules, and one draw needn't show every extreme that they name: `dest_block`: in the rows of one device (aligned blocks of 64 windows), no block index is named by more than 16 windows.
All inputs are finite; a program needn't handle non-finite values.
Results may differ from a plain program's by a relative error of at most 0.0003.
Values may be sent and summed in bfloat16 or wider, within the bound.
No kernel may reach another device: no remote copies, remote signals or barrier semaphores. Data moves between devices by JAX's collectives and lax.ppermute only.
A program may use at most 64 MiB of HBM per device.

v0:
```python
import math
import jax
import jax.numpy as jnp
from jax import lax
from jax.sharding import PartitionSpec as P

CHIP = 64
WIN = 128
GC = 8
precise = lax.Precision.HIGHEST
epsilon = 1e-06


def padded(block, sides, width):
    for axis, dim in sides:
        count = lax.axis_size(axis)
        forward = [(i, i + 1) for i in range(count - 1)]
        backward = [(target, source) for source, target in forward]
        low = lax.ppermute(
            lax.slice_in_dim(block, block.shape[dim] - width, None, axis=dim), axis, forward
        )
        high = lax.ppermute(lax.slice_in_dim(block, 0, width, axis=dim), axis, backward)
        block = jnp.concatenate([low, block, high], axis=dim)
    return block


def tables(length, width):
    freqs = jnp.arange(length, dtype=jnp.int32)[:, None]
    places = jnp.arange(width, dtype=jnp.int32)[None, :]
    phase = freqs * places % length
    angle = phase.astype(jnp.float32) * (2.0 * math.pi / length)
    return (jnp.cos(angle), jnp.sin(angle))


def spectrum(image, cosine, sine_table):
    first_real = jnp.einsum("kn,bnm->bkm", cosine, image, precision=precise)
    first_imag = -jnp.einsum("kn,bnm->bkm", sine_table, image, precision=precise)
    spec_real = jnp.einsum("bkm,lm->bkl", first_real, cosine, precision=precise) + jnp.einsum(
        "bkm,lm->bkl", first_imag, sine_table, precision=precise
    )
    spec_imag = jnp.einsum("bkm,lm->bkl", first_imag, cosine, precision=precise) - jnp.einsum(
        "bkm,lm->bkl", first_real, sine_table, precision=precise
    )
    return (spec_real, spec_imag)


def centre(chips_raw, chip_side):
    chip_float = chips_raw.astype(jnp.float32).reshape(-1, chip_side, chip_side)
    centred = chip_float - jnp.mean(chip_float, axis=(1, 2), keepdims=True)
    chip_std = jnp.sqrt(jnp.mean(centred * centred, axis=(1, 2)) + epsilon)
    return (centred, chip_std)


def match(chip_real, chip_imag, chip_std, windows_raw, chip_side, window_side):
    offsets = window_side - chip_side
    cos_full, sin_full = tables(window_side, window_side)
    cos_part = cos_full[:offsets]
    sin_part = sin_full[:offsets]
    window_float = windows_raw.astype(jnp.float32).reshape(-1, window_side, window_side)
    win_real, win_imag = spectrum(window_float, cos_full, sin_full)
    product_real = chip_real * win_real + chip_imag * win_imag
    product_imag = chip_real * win_imag - chip_imag * win_real
    half_real = jnp.einsum("ak,bkl->bal", cos_part, product_real, precision=precise) - jnp.einsum(
        "ak,bkl->bal", sin_part, product_imag, precision=precise
    )
    half_imag = jnp.einsum("ak,bkl->bal", cos_part, product_imag, precision=precise) + jnp.einsum(
        "ak,bkl->bal", sin_part, product_real, precision=precise
    )
    numerator = (
        jnp.einsum("bal,el->bae", half_real, cos_part, precision=precise)
        - jnp.einsum("bal,el->bae", half_imag, sin_part, precision=precise)
    ) / (window_side * window_side)
    starts = jnp.arange(offsets, dtype=jnp.int32)[:, None]
    pixels = jnp.arange(window_side, dtype=jnp.int32)[None, :]
    window_band = ((pixels >= starts) & (pixels < starts + chip_side)).astype(jnp.float32)
    first_rows = jnp.einsum("ax,bxy->bay", window_band, window_float, precision=precise)
    first_sum = jnp.einsum("bay,ey->bae", first_rows, window_band, precision=precise)
    second_rows = jnp.einsum(
        "ax,bxy->bay", window_band, window_float * window_float, precision=precise
    )
    second_sum = jnp.einsum("bay,ey->bae", second_rows, window_band, precision=precise)
    patch_mean = first_sum / (chip_side * chip_side)
    patch_var = second_sum / (chip_side * chip_side) - patch_mean * patch_mean
    score = numerator / (chip_side * chip_std[:, None, None] * jnp.sqrt(patch_var + epsilon))
    return score.reshape(-1, offsets * offsets)


def in_blocks(function, operands):
    amount = operands[0].shape[0]
    block_rows = 16
    shaped = tuple(
        (item.reshape((amount // block_rows, block_rows) + item.shape[1:]) for item in operands)
    )
    result = lax.map(lambda grouped: function(*grouped), shaped)
    return result.reshape(amount, -1)


def on_device(ref_chips, search_windows, dest_block, dest_slot):
    chips = ref_chips[0]
    windows = search_windows[0]
    targets = dest_block[0, :, 0]
    target_slot = dest_slot[0]
    chip_side = CHIP
    window_side = WIN
    offsets = window_side - chip_side
    window_amount = windows.shape[0]
    chip_amount = chips.shape[0]
    devices = lax.axis_size(("tile", "sub"))
    capacity = max(2, 2 * window_amount // devices)
    slot_amount = devices * capacity
    order = jnp.arange(window_amount, dtype=jnp.int32)
    matches = targets[:, None] == targets[None, :]
    earlier = order[:, None] > order[None, :]
    ranking = jnp.sum((matches & earlier).astype(jnp.int32), axis=1)
    positions = targets * capacity + ranking
    slot_buffer = jnp.full((slot_amount,), -1, jnp.int32).at[positions].set(target_slot)
    cos_chip, sin_chip = tables(window_side, chip_side)
    requests = slot_buffer.reshape(devices, capacity)
    found = jnp.take(
        chips,
        jnp.maximum(
            lax.all_to_all(requests, ("tile", "sub"), split_axis=0, concat_axis=0, tiled=True), 0
        ),
        axis=0,
    )
    fetched = lax.all_to_all(found, ("tile", "sub"), split_axis=0, concat_axis=0, tiled=True)
    own_chips = jnp.take(fetched.reshape(slot_amount, chip_side * chip_side), positions, axis=0)

    def match_own(chip_part, window_part):
        centred_part, std_part = centre(chip_part, chip_side)
        real_part, imag_part = spectrum(centred_part, cos_chip, sin_chip)
        return match(real_part, imag_part, std_part, window_part, chip_side, window_side)

    own_scores = in_blocks(match_own, (own_chips, windows))
    score_buffer = (
        jnp.zeros((slot_amount, offsets * offsets), jnp.float32).at[positions].set(own_scores)
    )
    scores, slots_here = (
        lax.all_to_all(score_buffer, ("tile", "sub"), split_axis=0, concat_axis=0, tiled=True),
        lax.all_to_all(slot_buffer, ("tile", "sub"), split_axis=0, concat_axis=0, tiled=True),
    )
    hits_table = (slots_here[None, :] == jnp.arange(chip_amount, dtype=jnp.int32)[:, None]).astype(
        jnp.float32
    )
    total = jnp.dot(hits_table, scores, precision=precise)
    looks = jnp.sum(hits_table, axis=1)
    average = total / jnp.maximum(looks, 1.0)[:, None]
    grid = average.reshape(-1, GC, offsets * offsets)
    extended = padded(grid, ((("tile", "sub"), 0),), 1)
    vertical = extended[:-2] + extended[2:]
    sideways = jnp.pad(grid, ((0, 0), (1, 1), (0, 0)))
    horizontal = sideways[:, :-2] + sideways[:, 2:]
    smoothed = (4.0 * grid + vertical + horizontal) / 8.0
    return smoothed.reshape(1, chip_amount, offsets * offsets)


def solution(mesh):
    return jax.shard_map(
        on_device,
        mesh=mesh,
        in_specs=(
            P(("groups", "pair"), ("tile", "sub"), None),
            P(("groups", "pair"), ("tile", "sub"), None),
            P(("groups", "pair"), ("tile", "sub"), None),
            P(("groups", "pair"), ("tile", "sub")),
        ),
        out_specs=P(("groups", "pair"), ("tile", "sub"), None),
        check_vma=False,
    )
```

profile of v0, /device:TPU:1, one launch (start us, length us, event | category | flops | bytes accessed | tf_op | source)
XLA Modules:
  0.0 226.2 jit_solution(14719844709658617581)
XLA Ops:
  2.6 11.0 %all_to_all.35 = s32[8,1,16]{2,1,0:T(1,128)S(1)} all-to-all(s32[8,1,16]{2,1,0:T(1,128)S(1)} %bitcast.236), channel_id=1, replica_groups=mesh['groups'=2,'tile'=4,'pair'=2,'sub'=2] {'tile','sub'}, dimensions={0} | all-to-all | bytes 1024 | tf_op jit(solution)/shard_map/all_to_all | solution.py:122
  16.1 4.2 %all-to-all-start.2 = ((bf16[8,16,4096]{2,1,0:T(8,128)(2,1)}), bf16[8,16,4096]{2,1,0:T(8,128)(2,1)S(1)}, u32[]{:S(2)}, u32[]{:S(2)}) async-start(bf16[8,16,4096]{2,1,0:T(8,128)(2,1)} %broadcast_select_fusion), calls=%async_computation.2 | async-start | bytes 2097152 | tf_op jit(solution)/shard_map/all_to_all | solution.py:126
  21.1 24.7 %all-to-all-done.2 = bf16[8,16,4096]{2,1,0:T(8,128)(2,1)S(1)} async-done(((bf16[8,16,4096]{2,1,0:T(8,128)(2,1)}), bf16[8,16,4096]{2,1,0:T(8,128)(2,1)S(1)}, u32[]{:S(2)}, u32[]{:S(2)}) %all-to-all-start.2) | async-done | bytes 1048608 | tf_op jit(solution)/shard_map/all_to_all | solution.py:126
  45.9 4.2 %all-to-all-start = ((s32[8,16,1]{1,2,0:T(1,128)}), s32[8,16,1]{1,2,0:T(1,128)S(1)}, u32[]{:S(2)}, u32[]{:S(2)}) async-start(s32[8,16,1]{1,2,0:T(1,128)} %bitcast.5), calls=%async_computation | async-start | bytes 8192 | tf_op jit(solution)/shard_map/all_to_all | solution.py:140
  51.0 109.2 %while.14 = (s32[]{:T(128)}, f32[4,16,4096]{2,1,0:T(8,128)S(1)}, bf16[4,16,4096]{2,1,0:T(8,128)(2,1)S(1)}, bf16[4,16,16384]{2,1,0:T(8,128)(2,1)}, s32[]{:T(128)}) while((s32[]{:T(128)}, f32[4,16,4096]{2,1,0:T(8,128)S(1)}, bf16[4,16,4096]{2,1,0:T(8,128)(2,1)S(1)}, bf16[4,16,16384]{2,1,0:T(8,128)(2,1)}, s32[]{:T(128)}) %tuple.39), condition=%wide.region_5.6_spmd.clone.clone, body=%wide.region_2.5_spmd.clone.clone.sunk | while | flops 4872994816 | bytes 46598104 | solution.py:94
  58.1 2.0 fusion.248
  60.1 1.9 convolution_add_fusion.5
  62.1 1.9 fusion.252
  64.0 1.9 convolution_subtract_fusion.5
  85.4 2.0 fusion.248
  87.4 1.9 convolution_add_fusion.5
  89.3 1.9 fusion.252
  91.3 1.9 convolution_subtract_fusion.5
  112.7 2.0 fusion.248
  114.6 1.9 convolution_add_fusion.5
  118.5 1.9 convolution_subtract_fusion.5
  139.9 2.0 fusion.248
  141.9 1.9 convolution_add_fusion.5
  145.8 1.9 convolution_subtract_fusion.5
  160.3 2.6 %scatter_custom_fusion.1 = f32[128,4096]{1,0:T(8,128)} fusion(s32[64]{0:T(128)S(1)} %fusion.136, f32[64,4096]{1,0:T(8,128)S(1)} %bitcast.237, f32[]{:T(128)} %constant.141.clone.1), kind=kCustom, calls=%fused_computation.150 | custom fusion | bytes 2097156 | tf_op jit(solution)/shard_map/scatter | solution.py:136
  162.9 5.1 %all-to-all-start.3 = ((f32[8,16,4096]{2,1,0:T(8,128)}), f32[8,16,4096]{2,1,0:T(8,128)S(1)}, u32[]{:S(2)}, u32[]{:S(2)}) async-start(f32[8,16,4096]{2,1,0:T(8,128)} %bitcast.15), calls=%async_computation.3 | async-start | bytes 4194304 | tf_op jit(solution)/shard_map/all_to_all | solution.py:139
  169.4 46.7 %all-to-all-done.3 = f32[8,16,4096]{2,1,0:T(8,128)S(1)} async-done(((f32[8,16,4096]{2,1,0:T(8,128)}), f32[8,16,4096]{2,1,0:T(8,128)S(1)}, u32[]{:S(2)}, u32[]{:S(2)}) %all-to-all-start.3) | async-done | bytes 2097184 | tf_op jit(solution)/shard_map/all_to_all | solution.py:139
  218.9 2.4 %collective-permute-start.1 = (f32[1,8,4096]{2,1,0:T(8,128)S(1)}, f32[1,8,4096]{2,1,0:T(8,128)S(1)}, u32[]{:S(2)}, u32[]{:S(2)}) collective-permute-start(f32[1,8,4096]{2,1,0:T(8,128)S(1)} %get-tuple-element.139), channel_id=1, source_target_pairs={{1,0},{4,1},{5,4},{8,5},{9,8},{12,9},{13,12},{3,2},{6,3},{7,6},{10... | collective-permute-start | bytes 393224 | tf_op jit(solution)/shard_map/ppermute | solution.py:22
  221.3 3.9 %collective-permute-done.1 = f32[1,8,4096]{2,1,0:T(8,128)S(1)} collective-permute-done((f32[1,8,4096]{2,1,0:T(8,128)S(1)}, f32[1,8,4096]{2,1,0:T(8,128)S(1)}, u32[]{:S(2)}, u32[]{:S(2)}) %collective-permute-start.1) | collective-permute-done | bytes 131104 | tf_op jit(solution)/shard_map/ppermute | solution.py:22
  (164 shorter events, 92.8 us)
Async XLA Ops:
  0.0 13.7 %copy-start = (bf16[1,32,4096]{2,1,0:T(8,128)(2,1)S(1)}, bf16[1,32,4096]{2,1,0:T(8,128)(2,1)}, u32[]{:S(2)}) copy-start(bf16[1,32,4096]{2,1,0:T(8,128)(2,1)} %param.6) | copy-start | bytes 786436
  14.9 6.1 %copy-start.1 = (s32[1,64,1]{1,2,0:T(1,128)S(1)}, s32[1,64,1]{1,2,0:T(1,128)}, u32[]{:S(2)}) copy-start(s32[1,64,1]{1,2,0:T(1,128)} %param.8) | copy-start | bytes 772
  16.1 29.8 %all-to-all-start.2 = ((bf16[8,16,4096]{2,1,0:T(8,128)(2,1)}), bf16[8,16,4096]{2,1,0:T(8,128)(2,1)S(1)}, u32[]{:S(2)}, u32[]{:S(2)}) async-start(bf16[8,16,4096]{2,1,0:T(8,128)(2,1)} %broadcast_select_fusion), calls=%async_computation.2 | async-start | bytes 2097152 | tf_op jit(solution)/shard_map/all_to_all | solution.py:126
  45.9 117.0 %all-to-all-start = ((s32[8,16,1]{1,2,0:T(1,128)}), s32[8,16,1]{1,2,0:T(1,128)S(1)}, u32[]{:S(2)}, u32[]{:S(2)}) async-start(s32[8,16,1]{1,2,0:T(1,128)} %bitcast.5), calls=%async_computation | async-start | bytes 8192 | tf_op jit(solution)/shard_map/all_to_all | solution.py:140
  162.9 53.2 %all-to-all-start.3 = ((f32[8,16,4096]{2,1,0:T(8,128)}), f32[8,16,4096]{2,1,0:T(8,128)S(1)}, u32[]{:S(2)}, u32[]{:S(2)}) async-start(f32[8,16,4096]{2,1,0:T(8,128)} %bitcast.15), calls=%async_computation.3 | async-start | bytes 4194304 | tf_op jit(solution)/shard_map/all_to_all | solution.py:139
  217.0 4.3 %collective-permute-start = (f32[1,8,4096]{2,1,0:T(8,128)S(1)}, f32[1,8,4096]{2,1,0:T(8,128)S(1)}, u32[]{:S(2)}, u32[]{:S(2)}) collective-permute-start(f32[1,8,4096]{2,1,0:T(8,128)S(1)} %get-tuple-element.138), channel_id=1, source_target_pairs={{0,1},{1,4},{4,5},{5,8},{8,9},{9,12},{12,13},{2,3},{3,6},{6,7},{7,... | collective-permute-start | bytes 393224 | tf_op jit(solution)/shard_map/ppermute | solution.py:19
  218.9 6.3 %collective-permute-start.1 = (f32[1,8,4096]{2,1,0:T(8,128)S(1)}, f32[1,8,4096]{2,1,0:T(8,128)S(1)}, u32[]{:S(2)}, u32[]{:S(2)}) collective-permute-start(f32[1,8,4096]{2,1,0:T(8,128)S(1)} %get-tuple-element.139), channel_id=1, source_target_pairs={{1,0},{4,1},{5,4},{8,5},{9,8},{12,9},{13,12},{3,2},{6,3},{7,6},{10... | collective-permute-start | bytes 393224 | tf_op jit(solution)/shard_map/ppermute | solution.py:22
where the time goes:
time: 227 us; the launch traced here: 226 us
  matrix products  98 us (43%)
  waiting for transfers between devices  75.3 us (33%)
  starting transfers between devices  17.8 us (8%)
  local copies, waits for them, and re-layouts  14.4 us (6%)
  blocking collectives  11 us (5%)
  other arithmetic  8.43 us (4%)
    all_to_all x1, waiting for transfers between devices, on_device(): lax.all_to_all(score_buffer, ('tile', 'sub'), split_axis=0, concat_axis=0...  46.7 us
    all_to_all x1, waiting for transfers between devices, on_device(): lax.all_to_all(found, ('tile', 'sub'), split_axis=0, concat_axis=0, tiled...  24.7 us
    dot_general x8, matrix products, spectrum(): jnp.einsum('bkm,lm->bkl', first_real, sine_table, precision=precise)  15.5 us
    dot_general x8, matrix products, spectrum(): jnp.einsum('bkm,lm->bkl', first_real, cosine, precision=precise)  15.1 us
    dot_general x8, matrix products, spectrum(): jnp.einsum('bkm,lm->bkl', first_imag, sine_table, precision=precise)  15.1 us
    dot_general x8, matrix products, spectrum(): jnp.einsum('bkm,lm->bkl', first_imag, cosine, precision=precise)  15 us
    all_to_all x1, blocking collectives, on_device(): lax.all_to_all(requests, ('tile', 'sub'), split_axis=0, concat_axis=0, ti...  11 us
    dot_general x8, matrix products, spectrum(): first_real = jnp.einsum('kn,bnm->bkm', cosine, image, precision=precise)  6.31 us
  transfers between devices with their start and end apart: 5, of which 3 were waited for; matrix products, arithmetic and copies ran while one was open for 50% of the time, Pallas kernels for 0%

commit v1 on v0

--- a/solution.py
+++ b/solution.py
@@ -9,6 +9,20 @@
 GC = 8
 precise = lax.Precision.HIGHEST
 epsilon = 1e-06
+
+
+def order_page(mine, dim_k, mine_x):
+    local_part = mine.shape
+    d_next = mine.reshape(
+        *local_part[:dim_k], mine_x, local_part[dim_k] // mine_x, *local_part[dim_k + 1 :]
+    )
+    return jnp.moveaxis(d_next, dim_k, 0)
+
+
+def unite_the_sizes(panel, along_dim):
+    r2 = list(panel.shape[1:])
+    r2[along_dim] *= panel.shape[0]
+    return jnp.moveaxis(panel, 0, along_dim).reshape(r2)
 
 
 def padded(block, sides, width):
@@ -123,7 +137,17 @@
         ),
         axis=0,
     )
-    fetched = lax.all_to_all(found, ("tile", "sub"), split_axis=0, concat_axis=0, tiled=True)
+    finding, found_now = (lax.axis_size(("tile", "sub")), lax.axis_index(("tile", "sub")))
+    y_new = order_page(found, 0, finding)
+    answer = y_new
+    for j0 in tuple(range(1, finding)):
+        tmp, state_next = ((found_now + j0) % finding, (found_now - j0) % finding)
+        b_now = lax.dynamic_index_in_dim(y_new, tmp, 0)
+        before = lax.ppermute(
+            b_now, ("tile", "sub"), [(w, (w + j0) % finding) for w in range(finding)]
+        )
+        answer = lax.dynamic_update_slice_in_dim(answer, before, state_next, axis=0)
+    fetched = unite_the_sizes(answer, 0)
     own_chips = jnp.take(fetched.reshape(slot_amount, chip_side * chip_side), positions, axis=0)
 
     def match_own(chip_part, window_part):

time: 227 us -> 224 us (0.987)
  starting transfers between devices: 17.8 us -> 35.1 us
  blocking collectives: 11 us -> 0 us
  waiting for transfers between devices: 75.3 us -> 65.6 us
    all_to_all x1, waiting for transfers between devices: 24.7 us -> 3.28 us  [on_device(): lax.all_to_all(requests, ('tile', 'sub'), split_axis=0, concat_axis=0, ti...]
    ppermute x0 -> x7, starting transfers between devices: none -> 15.6 us  [on_device(): lax.ppermute(b_now, ('tile', 'sub'), [(w, (w + j0) % finding) for w in ra...]
    ppermute x0 -> x7, waiting for transfers between devices: none -> 11.7 us  [on_device(): lax.ppermute(b_now, ('tile', 'sub'), [(w, (w + j0) % finding) for w in ra...]
    all_to_all x1 -> x0, blocking collectives: 11 us -> none  [on_device(): lax.all_to_all(requests, ('tile', 'sub'), split_axis=0, concat_axis=0, ti...]
  transfers between devices with their start and end apart: 5 -> 12, of which waited for: 3 -> 5; matrix products, arithmetic and copies ran while one was open for 50% -> 52% of each run, Pallas kernels for 0% -> 0%
where the time goes in v1:
time: 224 us
  matrix products  98 us (44%)
  waiting for transfers between devices  65.6 us (29%)
  starting transfers between devices  35.1 us (16%)
  local copies, waits for them, and re-layouts  15.1 us (7%)
  other arithmetic  8.25 us (4%)
    all_to_all x1, waiting for transfers between devices, on_device(): lax.all_to_all(score_buffer, ('tile', 'sub'), split_axis=0, concat_axis=0...  46.7 us
    ppermute x7, starting transfers between devices, on_device(): lax.ppermute(b_now, ('tile', 'sub'), [(w, (w + j0) % finding) for w in ra...  15.6 us
    dot_general x8, matrix products, spectrum(): jnp.einsum('bkm,lm->bkl', first_real, sine_table, precision=precise)  15.5 us
    dot_general x8, matrix products, spectrum(): jnp.einsum('bkm,lm->bkl', first_real, cosine, precision=precise)  15.1 us
    dot_general x8, matrix products, spectrum(): jnp.einsum('bkm,lm->bkl', first_imag, sine_table, precision=precise)  15.1 us
    dot_general x8, matrix products, spectrum(): jnp.einsum('bkm,lm->bkl', first_imag, cosine, precision=precise)  15 us
    ppermute x7, waiting for transfers between devices, on_device(): lax.ppermute(b_now, ('tile', 'sub'), [(w, (w + j0) % finding) for w in ra...  11.7 us
    all_to_all x1, starting transfers between devices, on_device(): lax.all_to_all(requests, ('tile', 'sub'), split_axis=0, concat_axis=0, ti...  6.37 us
  transfers between devices with their start and end apart: 12, of which 5 were waited for; matrix products, arithmetic and copies ran while one was open for 52% of the time, Pallas kernels for 0%

profile of v1, /device:TPU:1, one launch (start us, length us, event | category | flops | bytes accessed | tf_op | source)
XLA Modules:
  0.0 223.7 jit_solution(16707251174720662178)
XLA Ops:
  3.2 6.4 %all-to-all-start.1 = ((s32[8,1,16]{2,1,0:T(1,128)}), s32[8,1,16]{2,1,0:T(1,128)S(1)}, u32[]{:S(2)}, u32[]{:S(2)}) async-start(s32[8,1,16]{2,1,0:T(1,128)} %bitcast.6), calls=%async_computation.1 | async-start | bytes 8192 | tf_op jit(solution)/shard_map/all_to_all | solution.py:136
  11.1 3.3 %all-to-all-done.1 = s32[8,1,16]{2,1,0:T(1,128)S(1)} async-done(((s32[8,1,16]{2,1,0:T(1,128)}), s32[8,1,16]{2,1,0:T(1,128)S(1)}, u32[]{:S(2)}, u32[]{:S(2)}) %all-to-all-start.1) | async-done | bytes 544 | tf_op jit(solution)/shard_map/all_to_all | solution.py:136
  14.3 3.9 %all-to-all-start = ((s32[8,16,1]{1,2,0:T(1,128)}), s32[8,16,1]{1,2,0:T(1,128)S(1)}, u32[]{:S(2)}, u32[]{:S(2)}) async-start(s32[8,16,1]{1,2,0:T(1,128)} %bitcast.5), calls=%async_computation | async-start | bytes 8192 | tf_op jit(solution)/shard_map/all_to_all | solution.py:164
  21.7 2.0 collective-permute-start.5
  23.8 2.1 collective-permute-start.4
  27.0 9.8 %collective-permute-done.1 = bf16[1,1,16,4096]{3,2,0,1:T(8,128)(2,1)S(1)} collective-permute-done((bf16[1,1,16,4096]{3,2,0,1:T(8,128)(2,1)S(1)}, bf16[1,1,16,4096]{3,2,0,1:T(8,128)(2,1)S(1)}, u32[]{:S(2)}, u32[]{:S(2)}) %collective-permute-start.1) | collective-permute-done | bytes 131104 | tf_op jit(solution)/shard_map/ppermute | solution.py:146
  36.8 8.5 %collective-permute-start.2 = (bf16[1,1,16,4096]{3,2,0,1:T(8,128)(2,1)S(1)}, bf16[1,1,16,4096]{3,2,0,1:T(8,128)(2,1)S(1)}, u32[]{:S(2)}, u32[]{:S(2)}) collective-permute-start(bf16[1,1,16,4096]{3,2,0,1:T(8,128)(2,1)S(1)} %get-tuple-element.142), channel_id=1, source_target_pairs={{0,5},{1,8},{4,9},{5,12},{8,13},{9,0},{12,1},{13,4},{2,7},{3,10},{... | collective-permute-start | bytes 393224 | tf_op jit(solution)/shard_map/ppermute | solution.py:146
  48.4 109.4 %while.14 = (s32[]{:T(128)}, f32[4,16,4096]{2,1,0:T(8,128)S(1)}, bf16[4,16,4096]{2,1,0:T(8,128)(2,1)S(1)}, bf16[4,16,16384]{2,1,0:T(8,128)(2,1)}, s32[]{:T(128)}) while((s32[]{:T(128)}, f32[4,16,4096]{2,1,0:T(8,128)S(1)}, bf16[4,16,4096]{2,1,0:T(8,128)(2,1)S(1)}, bf16[4,16,16384]{2,1,0:T(8,128)(2,1)}, s32[]{:T(128)}) %tuple.45), condition=%wide.region_5.6_spmd.clone.clone, body=%wide.region_2.5_spmd.clone.clone.sunk | while | flops 4872994816 | bytes 46598104 | solution.py:108
  55.7 2.0 fusion.248
  57.7 1.9 convolution_add_fusion.5
  61.6 1.9 convolution_subtract_fusion.5
  83.0 2.0 fusion.248
  84.9 1.9 convolution_add_fusion.5
  88.8 1.9 convolution_subtract_fusion.5
  110.2 2.0 fusion.248
  112.2 1.9 convolution_add_fusion.5
  116.1 1.9 convolution_subtract_fusion.5
  137.5 2.0 fusion.248
  139.4 1.9 convolution_add_fusion.5
  157.9 2.6 %scatter_custom_fusion.1 = f32[128,4096]{1,0:T(8,128)} fusion(s32[64]{0:T(128)S(1)} %fusion.136, f32[64,4096]{1,0:T(8,128)S(1)} %bitcast.252, f32[]{:T(128)} %constant.239.clone.1), kind=kCustom, calls=%fused_computation.150 | custom fusion | bytes 2097156 | tf_op jit(solution)/shard_map/scatter | solution.py:160
  160.5 5.0 %all-to-all-start.2 = ((f32[8,16,4096]{2,1,0:T(8,128)}), f32[8,16,4096]{2,1,0:T(8,128)S(1)}, u32[]{:S(2)}, u32[]{:S(2)}) async-start(f32[8,16,4096]{2,1,0:T(8,128)} %bitcast.23), calls=%async_computation.2 | async-start | bytes 4194304 | tf_op jit(solution)/shard_map/all_to_all | solution.py:163
  166.9 46.7 %all-to-all-done.2 = f32[8,16,4096]{2,1,0:T(8,128)S(1)} async-done(((f32[8,16,4096]{2,1,0:T(8,128)}), f32[8,16,4096]{2,1,0:T(8,128)S(1)}, u32[]{:S(2)}, u32[]{:S(2)}) %all-to-all-start.2) | async-done | bytes 2097184 | tf_op jit(solution)/shard_map/all_to_all | solution.py:163
  216.4 2.4 %collective-permute-start.8 = (f32[1,8,4096]{2,1,0:T(8,128)S(1)}, f32[1,8,4096]{2,1,0:T(8,128)S(1)}, u32[]{:S(2)}, u32[]{:S(2)}) collective-permute-start(f32[1,8,4096]{2,1,0:T(8,128)S(1)} %get-tuple-element.146), channel_id=1, source_target_pairs={{1,0},{4,1},{5,4},{8,5},{9,8},{12,9},{13,12},{3,2},{6,3},{7,6},{10... | collective-permute-start | bytes 393224 | tf_op jit(solution)/shard_map/ppermute | solution.py:36
  218.8 3.9 %collective-permute-done.8 = f32[1,8,4096]{2,1,0:T(8,128)S(1)} collective-permute-done((f32[1,8,4096]{2,1,0:T(8,128)S(1)}, f32[1,8,4096]{2,1,0:T(8,128)S(1)}, u32[]{:S(2)}, u32[]{:S(2)}) %collective-permute-start.8) | collective-permute-done | bytes 131104 | tf_op jit(solution)/shard_map/ppermute | solution.py:36
  (184 shorter events, 104.1 us)
Async XLA Ops:
  0.0 18.3 %copy-start = (bf16[1,32,4096]{2,1,0:T(8,128)(2,1)S(1)}, bf16[1,32,4096]{2,1,0:T(8,128)(2,1)}, u32[]{:S(2)}) copy-start(bf16[1,32,4096]{2,1,0:T(8,128)(2,1)} %param.6) | copy-start | bytes 786436
  3.2 11.2 %all-to-all-start.1 = ((s32[8,1,16]{2,1,0:T(1,128)}), s32[8,1,16]{2,1,0:T(1,128)S(1)}, u32[]{:S(2)}, u32[]{:S(2)}) async-start(s32[8,1,16]{2,1,0:T(1,128)} %bitcast.6), calls=%async_computation.1 | async-start | bytes 8192 | tf_op jit(solution)/shard_map/all_to_all | solution.py:136
  14.3 146.1 %all-to-all-start = ((s32[8,16,1]{1,2,0:T(1,128)}), s32[8,16,1]{1,2,0:T(1,128)S(1)}, u32[]{:S(2)}, u32[]{:S(2)}) async-start(s32[8,16,1]{1,2,0:T(1,128)} %bitcast.5), calls=%async_computation | async-start | bytes 8192 | tf_op jit(solution)/shard_map/all_to_all | solution.py:164
  19.8 6.7 %collective-permute-start = (bf16[1,1,16,4096]{3,2,0,1:T(8,128)(2,1)S(1)}, bf16[1,1,16,4096]{3,2,0,1:T(8,128)(2,1)S(1)}, u32[]{:S(2)}, u32[]{:S(2)}) collective-permute-start(bf16[1,1,16,4096]{3,2,0,1:T(8,128)(2,1)S(1)} %get-tuple-element.144), channel_id=1, source_target_pairs={{0,1},{1,4},{4,5},{5,8},{8,9},{9,12},{12,13},{13,0},{2,3},{3,6},{6... | collective-permute-start | bytes 393224 | tf_op jit(solution)/shard_map/ppermute | solution.py:146
  21.6 25.8 %collective-permute-start.6 = (bf16[1,1,16,4096]{3,2,0,1:T(8,128)(2,1)S(1)}, bf16[1,1,16,4096]{3,2,0,1:T(8,128)(2,1)S(1)}, u32[]{:S(2)}, u32[]{:S(2)}) collective-permute-start(bf16[1,1,16,4096]{3,2,0,1:T(8,128)(2,1)S(1)} %get-tuple-element.138), channel_id=1, source_target_pairs={{0,13},{1,0},{4,1},{5,4},{8,5},{9,8},{12,9},{13,12},{2,15},{3,2},{... | collective-permute-start | bytes 393224 | tf_op jit(solution)/shard_map/ppermute | solution.py:146
  21.7 25.7 %collective-permute-start.5 = (bf16[1,1,16,4096]{3,2,0,1:T(8,128)(2,1)S(1)}, bf16[1,1,16,4096]{3,2,0,1:T(8,128)(2,1)S(1)}, u32[]{:S(2)}, u32[]{:S(2)}) collective-permute-start(bf16[1,1,16,4096]{3,2,0,1:T(8,128)(2,1)S(1)} %get-tuple-element.139), channel_id=1, source_target_pairs={{0,12},{1,13},{4,0},{5,1},{8,4},{9,5},{12,8},{13,9},{2,14},{3,15},... | collective-permute-start | bytes 393224 | tf_op jit(solution)/shard_map/ppermute | solution.py:146
  23.8 23.6 %collective-permute-start.4 = (bf16[1,1,16,4096]{3,2,0,1:T(8,128)(2,1)S(1)}, bf16[1,1,16,4096]{3,2,0,1:T(8,128)(2,1)S(1)}, u32[]{:S(2)}, u32[]{:S(2)}) collective-permute-start(bf16[1,1,16,4096]{3,2,0,1:T(8,128)(2,1)S(1)} %get-tuple-element.140), channel_id=1, source_target_pairs={{0,9},{1,12},{4,13},{5,0},{8,1},{9,4},{12,5},{13,8},{2,11},{3,14},... | collective-permute-start | bytes 393224 | tf_op jit(solution)/shard_map/ppermute | solution.py:146
  25.8 21.5 %collective-permute-start.3 = (bf16[1,1,16,4096]{3,2,0,1:T(8,128)(2,1)S(1)}, bf16[1,1,16,4096]{3,2,0,1:T(8,128)(2,1)S(1)}, u32[]{:S(2)}, u32[]{:S(2)}) collective-permute-start(bf16[1,1,16,4096]{3,2,0,1:T(8,128)(2,1)S(1)} %get-tuple-element.141), channel_id=1, source_target_pairs={{0,8},{1,9},{4,12},{5,13},{8,0},{9,1},{12,4},{13,5},{2,10},{3,11},... | collective-permute-start | bytes 393224 | tf_op jit(solution)/shard_map/ppermute | solution.py:146
  26.5 10.3 %collective-permute-start.1 = (bf16[1,1,16,4096]{3,2,0,1:T(8,128)(2,1)S(1)}, bf16[1,1,16,4096]{3,2,0,1:T(8,128)(2,1)S(1)}, u32[]{:S(2)}, u32[]{:S(2)}) collective-permute-start(bf16[1,1,16,4096]{3,2,0,1:T(8,128)(2,1)S(1)} %get-tuple-element.143), channel_id=1, source_target_pairs={{0,4},{1,5},{4,8},{5,9},{8,12},{9,13},{12,0},{13,1},{2,6},{3,7},{6... | collective-permute-start | bytes 393224 | tf_op jit(solution)/shard_map/ppermute | solution.py:146
  36.8 10.5 %collective-permute-start.2 = (bf16[1,1,16,4096]{3,2,0,1:T(8,128)(2,1)S(1)}, bf16[1,1,16,4096]{3,2,0,1:T(8,128)(2,1)S(1)}, u32[]{:S(2)}, u32[]{:S(2)}) collective-permute-start(bf16[1,1,16,4096]{3,2,0,1:T(8,128)(2,1)S(1)} %get-tuple-element.142), channel_id=1, source_target_pairs={{0,5},{1,8},{4,9},{5,12},{8,13},{9,0},{12,1},{13,4},{2,7},{3,10},{... | collective-permute-start | bytes 393224 | tf_op jit(solution)/shard_map/ppermute | solution.py:146
  160.5 53.1 %all-to-all-start.2 = ((f32[8,16,4096]{2,1,0:T(8,128)}), f32[8,16,4096]{2,1,0:T(8,128)S(1)}, u32[]{:S(2)}, u32[]{:S(2)}) async-start(f32[8,16,4096]{2,1,0:T(8,128)} %bitcast.23), calls=%async_computation.2 | async-start | bytes 4194304 | tf_op jit(solution)/shard_map/all_to_all | solution.py:163
  214.5 4.3 %collective-permute-start.7 = (f32[1,8,4096]{2,1,0:T(8,128)S(1)}, f32[1,8,4096]{2,1,0:T(8,128)S(1)}, u32[]{:S(2)}, u32[]{:S(2)}) collective-permute-start(f32[1,8,4096]{2,1,0:T(8,128)S(1)} %get-tuple-element.145), channel_id=1, source_target_pairs={{0,1},{1,4},{4,5},{5,8},{8,9},{9,12},{12,13},{2,3},{3,6},{6,7},{7,... | collective-permute-start | bytes 393224 | tf_op jit(solution)/shard_map/ppermute | solution.py:33
  216.4 6.3 %collective-permute-start.8 = (f32[1,8,4096]{2,1,0:T(8,128)S(1)}, f32[1,8,4096]{2,1,0:T(8,128)S(1)}, u32[]{:S(2)}, u32[]{:S(2)}) collective-permute-start(f32[1,8,4096]{2,1,0:T(8,128)S(1)} %get-tuple-element.146), channel_id=1, source_target_pairs={{1,0},{4,1},{5,4},{8,5},{9,8},{12,9},{13,12},{3,2},{6,3},{7,6},{10... | collective-permute-start | bytes 393224 | tf_op jit(solution)/shard_map/ppermute | solution.py:36
